TPU v7x, 32 devices: a whole 2x2x4 slice. The times are simulated.
32 devices in a mesh: ctx: 8 (over z, core), dp: 4 (over y, x).
Axes of the slice: x: 2, y: 2, z: 4, core: 2. Of those that a mesh axis runs over, the one named last changes fastest.
Arguments:
- projected: bfloat16 [8, 2, 64, 3, 8192], P('ctx', None, None, None, 'dp'), may hold values from -36 to 36, as said below
- filters: float32 [3, 7, 512], P(None, None, 'dp'), may hold values from -0.5 to 1.4, as said below
- gain: float32 [8192], P('dp'), may hold values from 0.5 to 1.5
- doc_lengths: int32 [4], replicated, may hold values from 1 to 320, 1024 in all
Outputs:
- mixed: bfloat16 [8, 2, 64, 8192], P('ctx', None, None, 'dp')
Inputs may be any that keep to these rules, and one draw needn't show every extreme that they name: `doc_lengths`: each document holds 1 to 320 tokens, the longest exactly 320; the lengths sum to 1024. `projected`: entries are finite. `filters`: filter taps other than the last lie in -0.5 to 0.5; the last lies in 0.6 to 1.4.
All inputs are finite; a program needn't handle non-finite values.
Results may differ from a plain program's by a relative error of at most 0.004.
The roundings to bfloat16 on the way count: a program that leaves them out, or rounds other values in their place, can miss the bound.
Values may be sent and summed in bfloat16 or wider, within the bound.
A program may use at most 64 MiB of HBM per device.

v0:
```python
import jax
import jax.numpy as jnp
from jax import lax
from jax.sharding import PartitionSpec as P

HEAD_DIM = 128
REACH = 5


def extended(block, sides, width):
    for axis, dim in sides:
        count = lax.axis_size(axis)
        forward = [(i, i + 1) for i in range(count - 1)]
        backward = [(target, source) for source, target in forward]
        low = lax.ppermute(
            lax.slice_in_dim(block, block.shape[dim] - width, None, axis=dim), axis, forward
        )
        high = lax.ppermute(lax.slice_in_dim(block, 0, width, axis=dim), axis, backward)
        block = jnp.concatenate([low, block, high], axis=dim)
    return block


def shifted(block, axis, distance):
    devices = range(lax.axis_size(axis))
    route = [(i - distance, i) for i in devices if i - distance in devices]
    return lax.ppermute(block, axis, route)


def local(projected, filters, gain, doc_lengths):
    blocks = projected[0]
    stretch_len = blocks.shape[1]
    local_width = blocks.shape[3]
    ctx_count = lax.axis_size("ctx")
    ctx_place = lax.axis_index("ctx")
    rim_width = filters.shape[1] - 1
    is_last = ctx_place == ctx_count - 1
    rim_rows = jnp.concatenate(
        [blocks[1, stretch_len - rim_width :], blocks[0, stretch_len - rim_width :]], axis=0
    )
    padded = extended(rim_rows, (("ctx", 0),), rim_width)
    lower_rim = padded[:rim_width]
    upper_rim = jnp.where(is_last, blocks[0, stretch_len - rim_width :], padded[3 * rim_width :])
    joined = jnp.stack(
        [
            jnp.concatenate([lower_rim, blocks[0]], axis=0),
            jnp.concatenate([upper_rim, blocks[1]], axis=0),
        ]
    )
    wide_filters = jnp.repeat(filters, local_width // filters.shape[2], axis=2)
    tap_weights = jnp.transpose(wide_filters, (1, 0, 2))
    summed = jnp.zeros((2, stretch_len, 3, local_width), jnp.float32)
    for tap_index in range(rim_width + 1):
        summed = (
            summed
            + joined[:, tap_index : tap_index + stretch_len].astype(jnp.float32)
            * tap_weights[tap_index]
        )
    conv = summed.astype(jnp.bfloat16)
    kv_own = conv[:, :, 1:]
    starts = jnp.stack([ctx_place * stretch_len, (2 * ctx_count - 1 - ctx_place) * stretch_len])
    doc_ends = jnp.cumsum(doc_lengths)
    offsets = jnp.arange(stretch_len, dtype=jnp.int32)
    query_pos = starts[:, None] + offsets[None, :]

    def doc_of(positions):
        return jnp.sum((doc_ends <= positions[..., None]).astype(jnp.int32), axis=-1)

    query_doc = doc_of(query_pos)

    def mask_for(distance):
        key_pos = (starts - distance * stretch_len)[:, None] + offsets[None, :]
        allowed = (key_pos[:, None, :] <= query_pos[:, :, None]) & (key_pos[:, None, :] >= 0)
        return allowed & (query_doc[:, :, None] == doc_of(key_pos)[:, None, :])

    head_count = local_width // HEAD_DIM
    queries = conv[:, :, 0].reshape(2, stretch_len, head_count, HEAD_DIM)

    def tile(carry, kv_rows, key_mask):
        run_max, run_total, run_acc = carry
        keys_blk = kv_rows[:, :, 0].reshape(2, stretch_len, head_count, HEAD_DIM)
        values_blk = kv_rows[:, :, 1].reshape(2, stretch_len, head_count, HEAD_DIM)
        scores = jnp.einsum(
            "bqhd,bkhd->bhqk", queries, keys_blk, preferred_element_type=jnp.float32
        ) * HEAD_DIM ** (-0.5)
        scores = jnp.where(key_mask[:, None], scores, -1e30)
        new_max = jnp.maximum(run_max, jnp.max(scores, axis=-1, keepdims=True))
        rescale = jnp.exp(run_max - new_max)
        exp_terms = jnp.exp(scores - new_max)
        new_total = run_total * rescale + jnp.sum(exp_terms, axis=-1, keepdims=True)
        weights = exp_terms.astype(jnp.bfloat16)
        update = jnp.einsum(
            "bhqk,bkhd->bhqd", weights, values_blk, preferred_element_type=jnp.float32
        )
        return (new_max, new_total, run_acc * rescale + update)

    def tile_step(carry, kv_rows, key_mask):
        return tile(carry, kv_rows, key_mask)

    carry = (
        jnp.full((2, head_count, stretch_len, 1), -1e30, jnp.float32),
        jnp.zeros((2, head_count, stretch_len, 1), jnp.float32),
        jnp.zeros((2, head_count, stretch_len, HEAD_DIM), jnp.float32),
    )
    carry = tile_step(carry, kv_own, mask_for(0))
    lower_buf = kv_own[0]
    upper_buf = kv_own[1]
    for distance in range(1, REACH + 1):
        from_lower = shifted(lower_buf, "ctx", 1)
        from_upper = shifted(upper_buf, "ctx", -1)
        upper_buf = jnp.where(is_last, lower_buf, from_upper)
        lower_buf = from_lower
        carry = tile_step(carry, jnp.stack([lower_buf, upper_buf]), mask_for(distance))
    run_max, run_total, run_acc = carry
    attended = jnp.transpose(run_acc / run_total, (0, 2, 1, 3)).reshape(2, stretch_len, local_width)
    squares = jnp.sum(attended * attended, axis=-1)
    total_sq = lax.psum(squares, "dp")
    full_width = local_width * lax.axis_size("dp")
    mixed = (attended * lax.rsqrt(total_sq / full_width + 1e-06)[..., None] * gain).astype(
        jnp.bfloat16
    )
    return mixed[None]


def solution(mesh):
    in_specs = (P("ctx", None, None, None, "dp"), P(None, None, "dp"), P("dp"), P())
    out_specs = P("ctx", None, None, "dp")
    return jax.shard_map(local, mesh=mesh, in_specs=in_specs, out_specs=out_specs, check_vma=False)
```

profile of v0, /device:TPU:24, one launch (start us, length us, event | category | flops | bytes accessed | tf_op | source)
XLA Modules:
  0.0 95.1 jit_solution(5000069265065464107)
XLA Ops:
  0.0 1.0 %slice_bitcast_fusion.4 = (bf16[6,3,2048]{2,0,1:T(8,128)(2,1)S(1)}, bf16[6,3,2048]{2,0,1:T(8,128)(2,1)S(1)}) fusion(bf16[2,64,3,2048]{3,1,2,0:T(8,128)(2,1)} %bitcast.258), kind=kLoop, calls=%fused_computation.125 | loop fusion | bytes 294912 | tf_op jit(solution)/shard_map/squeeze | solution.py:38
  1.0 1.9 %collective-permute-start.1 = (bf16[6,3,2048]{2,0,1:T(8,128)(2,1)S(1)}, bf16[6,3,2048]{2,0,1:T(8,128)(2,1)S(1)}, u32[]{:S(2)}, u32[]{:S(2)}) collective-permute-start(bf16[6,3,2048]{2,0,1:T(8,128)(2,1)S(1)} %get-tuple-element.28), channel_id=1, source_target_pairs={{4,0},{8,4},{12,8},{16,12},{20,16},{24,20},{28,24},{5,1},{9,5},{13... | collective-permute-start | bytes 221192 | tf_op jit(solution)/shard_map/ppermute | solution.py:18
  2.9 2.4 %collective-permute-start = (bf16[6,3,2048]{2,0,1:T(8,128)(2,1)S(1)}, bf16[6,3,2048]{2,0,1:T(8,128)(2,1)S(1)}, u32[]{:S(2)}, u32[]{:S(2)}) collective-permute-start(bf16[6,3,2048]{2,0,1:T(8,128)(2,1)S(1)} %get-tuple-element.29), channel_id=1, source_target_pairs={{0,4},{4,8},{8,12},{12,16},{16,20},{20,24},{24,28},{1,5},{5,9},{9,... | collective-permute-start | bytes 221192 | tf_op jit(solution)/shard_map/ppermute | solution.py:15
  8.1 1.5 %slice_bitcast_fusion = (bf16[64,3,2048]{2,0,1:T(8,128)(2,1)S(1)}, bf16[64,3,2048]{2,0,1:T(8,128)(2,1)S(1)}) fusion(bf16[1,2,64,3,2048]{4,2,3,1,0:T(8,128)(2,1)} %param.4), kind=kLoop, calls=%fused_computation.82 | loop fusion | bytes 3145728 | tf_op jit(solution)/shard_map/squeeze | solution.py:46
  12.6 1.3 %compare_and_fusion.3 = (pred[2,64,64]{1,2,0:T(8,128)(4,1)S(1)}, pred[2,64,64]{1,2,0:T(8,128)(4,1)S(1)}, pred[2,64,64]{1,2,0:T(8,128)(4,1)S(1)}, pred[2,64,64]{1...) fusion(s32[2,64]{1,0:T(2,128)S(1)} %get-tuple-element.7, ...), kind=kLoop, calls=%fused_computation.131 | loop fusion | flops 196608 | bytes 56064 | tf_op jit(solution)/shard_map/and | solution.py:73
  15.4 3.1 %add_convert_fusion = bf16[2,64,3,2048]{3,1,2,0:T(8,128)(2,1)S(1)} fusion(bf16[1,70,3,2048]{3,1,2,0:T(8,128)(2,1)S(1)} %maximum_bitcast_fusion, bf16[1,70,3,2048]{3,1,2,0:T(8,128)(2,1)S(1)} %maximum_bitcast_fusion.1, f32[3,2048]{1,0:T(4,128)S(1)} %get-tuple-element.76, f32[3,2048]{1,0:T(4,128)S(1)} %get-tuple-element.77, f32[3,2048]{1,0:T(4,128)S(1)} %get-tuple-element.78, ...), kind=kLoop, calls=%fused_computation | loop fusion | flops 33030144 | bytes 3465216 | tf_op jit(solution)/shard_map/convert_element_type | solution.py:58
  18.6 3.2 %collective-permute-start.3 = (bf16[64,2,2048]{2,0,1:T(8,128)(2,1)S(1)}, bf16[64,2,2048]{2,0,1:T(8,128)(2,1)S(1)}, u32[]{:S(2)}, u32[]{:S(2)}) collective-permute-start(bf16[64,2,2048]{2,0,1:T(8,128)(2,1)S(1)} %get-tuple-element.23), channel_id=1, source_target_pairs={{4,0},{8,4},{12,8},{16,12},{20,16},{24,20},{28,24},{5,1},{9,5},{13... | collective-permute-start | bytes 1572872 | tf_op jit(solution)/shard_map/ppermute | solution.py:26
  22.1 1.9 %collective-permute-start.2 = (bf16[64,2,2048]{2,0,1:T(8,128)(2,1)S(1)}, bf16[64,2,2048]{2,0,1:T(8,128)(2,1)S(1)}, u32[]{:S(2)}, u32[]{:S(2)}) collective-permute-start(bf16[64,2,2048]{2,0,1:T(8,128)(2,1)S(1)} %get-tuple-element.24), channel_id=1, source_target_pairs={{0,4},{4,8},{8,12},{12,16},{16,20},{20,24},{24,28},{1,5},{5,9},{9,... | collective-permute-start | bytes 1572872 | tf_op jit(solution)/shard_map/ppermute | solution.py:26
  24.6 3.8 %collective-permute-done.3 = bf16[64,2,2048]{2,0,1:T(8,128)(2,1)S(1)} collective-permute-done((bf16[64,2,2048]{2,0,1:T(8,128)(2,1)S(1)}, bf16[64,2,2048]{2,0,1:T(8,128)(2,1)S(1)}, u32[]{:S(2)}, u32[]{:S(2)}) %collective-permute-start.3) | collective-permute-done | bytes 524320 | tf_op jit(solution)/shard_map/ppermute | solution.py:26
  28.5 4.1 %collective-permute-start.5 = (bf16[64,2,2048]{2,0,1:T(8,128)(2,1)S(1)}, bf16[64,2,2048]{2,0,1:T(8,128)(2,1)S(1)}, u32[]{:S(2)}, u32[]{:S(2)}) collective-permute-start(bf16[64,2,2048]{2,0,1:T(8,128)(2,1)S(1)} %broadcast_select_fusion.3), channel_id=1, source_target_pairs={{4,0},{8,4},{12,8},{16,12},{20,16},{24,20},{28,24},{5,1},{9,5},{13... | collective-permute-start | bytes 1572872 | tf_op jit(solution)/shard_map/ppermute | solution.py:26
  32.8 1.9 %collective-permute-start.4 = (bf16[64,2,2048]{2,0,1:T(8,128)(2,1)S(1)}, bf16[64,2,2048]{2,0,1:T(8,128)(2,1)S(1)}, u32[]{:S(2)}, u32[]{:S(2)}) collective-permute-start(bf16[64,2,2048]{2,0,1:T(8,128)(2,1)S(1)} %collective-permute-done.2), channel_id=1, source_target_pairs={{0,4},{4,8},{8,12},{12,16},{16,20},{20,24},{24,28},{1,5},{5,9},{9,... | collective-permute-start | bytes 1572872 | tf_op jit(solution)/shard_map/ppermute | solution.py:26
  35.3 4.0 %collective-permute-done.5 = bf16[64,2,2048]{2,0,1:T(8,128)(2,1)S(1)} collective-permute-done((bf16[64,2,2048]{2,0,1:T(8,128)(2,1)S(1)}, bf16[64,2,2048]{2,0,1:T(8,128)(2,1)S(1)}, u32[]{:S(2)}, u32[]{:S(2)}) %collective-permute-start.5) | collective-permute-done | bytes 524320 | tf_op jit(solution)/shard_map/ppermute | solution.py:26
  39.3 4.1 %collective-permute-start.7 = (bf16[64,2,2048]{2,0,1:T(8,128)(2,1)S(1)}, bf16[64,2,2048]{2,0,1:T(8,128)(2,1)S(1)}, u32[]{:S(2)}, u32[]{:S(2)}) collective-permute-start(bf16[64,2,2048]{2,0,1:T(8,128)(2,1)S(1)} %broadcast_select_fusion.2), channel_id=1, source_target_pairs={{4,0},{8,4},{12,8},{16,12},{20,16},{24,20},{28,24},{5,1},{9,5},{13... | collective-permute-start | bytes 1572872 | tf_op jit(solution)/shard_map/ppermute | solution.py:26
  43.7 1.9 %collective-permute-start.6 = (bf16[64,2,2048]{2,0,1:T(8,128)(2,1)S(1)}, bf16[64,2,2048]{2,0,1:T(8,128)(2,1)S(1)}, u32[]{:S(2)}, u32[]{:S(2)}) collective-permute-start(bf16[64,2,2048]{2,0,1:T(8,128)(2,1)S(1)} %collective-permute-done.4), channel_id=1, source_target_pairs={{0,4},{4,8},{8,12},{12,16},{16,20},{20,24},{24,28},{1,5},{5,9},{9,... | collective-permute-start | bytes 1572872 | tf_op jit(solution)/shard_map/ppermute | solution.py:26
  46.2 4.0 %collective-permute-done.7 = bf16[64,2,2048]{2,0,1:T(8,128)(2,1)S(1)} collective-permute-done((bf16[64,2,2048]{2,0,1:T(8,128)(2,1)S(1)}, bf16[64,2,2048]{2,0,1:T(8,128)(2,1)S(1)}, u32[]{:S(2)}, u32[]{:S(2)}) %collective-permute-start.7) | collective-permute-done | bytes 524320 | tf_op jit(solution)/shard_map/ppermute | solution.py:26
  50.2 4.1 %collective-permute-start.9 = (bf16[64,2,2048]{2,0,1:T(8,128)(2,1)S(1)}, bf16[64,2,2048]{2,0,1:T(8,128)(2,1)S(1)}, u32[]{:S(2)}, u32[]{:S(2)}) collective-permute-start(bf16[64,2,2048]{2,0,1:T(8,128)(2,1)S(1)} %broadcast_select_fusion.1), channel_id=1, source_target_pairs={{4,0},{8,4},{12,8},{16,12},{20,16},{24,20},{28,24},{5,1},{9,5},{13... | collective-permute-start | bytes 1572872 | tf_op jit(solution)/shard_map/ppermute | solution.py:26
  54.5 1.9 %collective-permute-start.8 = (bf16[64,2,2048]{2,0,1:T(8,128)(2,1)S(1)}, bf16[64,2,2048]{2,0,1:T(8,128)(2,1)S(1)}, u32[]{:S(2)}, u32[]{:S(2)}) collective-permute-start(bf16[64,2,2048]{2,0,1:T(8,128)(2,1)S(1)} %collective-permute-done.6), channel_id=1, source_target_pairs={{0,4},{4,8},{8,12},{12,16},{16,20},{20,24},{24,28},{1,5},{5,9},{9,... | collective-permute-start | bytes 1572872 | tf_op jit(solution)/shard_map/ppermute | solution.py:26
  57.0 4.0 %collective-permute-done.9 = bf16[64,2,2048]{2,0,1:T(8,128)(2,1)S(1)} collective-permute-done((bf16[64,2,2048]{2,0,1:T(8,128)(2,1)S(1)}, bf16[64,2,2048]{2,0,1:T(8,128)(2,1)S(1)}, u32[]{:S(2)}, u32[]{:S(2)}) %collective-permute-start.9) | collective-permute-done | bytes 524320 | tf_op jit(solution)/shard_map/ppermute | solution.py:26
  61.0 4.1 %collective-permute-start.11 = (bf16[64,2,2048]{2,0,1:T(8,128)(2,1)S(1)}, bf16[64,2,2048]{2,0,1:T(8,128)(2,1)S(1)}, u32[]{:S(2)}, u32[]{:S(2)}) collective-permute-start(bf16[64,2,2048]{2,0,1:T(8,128)(2,1)S(1)} %broadcast_select_fusion), channel_id=1, source_target_pairs={{4,0},{8,4},{12,8},{16,12},{20,16},{24,20},{28,24},{5,1},{9,5},{13... | collective-permute-start | bytes 1572872 | tf_op jit(solution)/shard_map/ppermute | solution.py:26
  65.4 2.1 %collective-permute-start.10 = (bf16[64,2,2048]{2,0,1:T(8,128)(2,1)S(1)}, bf16[64,2,2048]{2,0,1:T(8,128)(2,1)S(1)}, u32[]{:S(2)}, u32[]{:S(2)}) collective-permute-start(bf16[64,2,2048]{2,0,1:T(8,128)(2,1)S(1)} %collective-permute-done.8), channel_id=1, source_target_pairs={{0,4},{4,8},{8,12},{12,16},{16,20},{20,24},{24,28},{1,5},{5,9},{9,... | collective-permute-start | bytes 1572872 | tf_op jit(solution)/shard_map/ppermute | solution.py:26
  68.1 3.8 %collective-permute-done.11 = bf16[64,2,2048]{2,0,1:T(8,128)(2,1)S(1)} collective-permute-done((bf16[64,2,2048]{2,0,1:T(8,128)(2,1)S(1)}, bf16[64,2,2048]{2,0,1:T(8,128)(2,1)S(1)}, u32[]{:S(2)}, u32[]{:S(2)}) %collective-permute-start.11) | collective-permute-done | bytes 524320 | tf_op jit(solution)/shard_map/ppermute | solution.py:26
  71.9 4.0 %collective-permute-done.10 = bf16[64,2,2048]{2,0,1:T(8,128)(2,1)S(1)} collective-permute-done((bf16[64,2,2048]{2,0,1:T(8,128)(2,1)S(1)}, bf16[64,2,2048]{2,0,1:T(8,128)(2,1)S(1)}, u32[]{:S(2)}, u32[]{:S(2)}) %collective-permute-start.10) | collective-permute-done | bytes 524320 | tf_op jit(solution)/shard_map/ppermute | solution.py:26
  78.1 1.3 %fusion.17 = f32[2,64,16,128]{3,1,2,0:T(8,128)S(1)} fusion(f32[2,16,64,64]{2,3,1,0:T(8,128)S(1)} %get-tuple-element.73, bf16[2,64,16,128]{3,2,1,0:T(8,128)(2,1)S(1)} %bitcast.264, f32[2,64,16]{1,2,0:T(8,128)S(1)} %get-tuple-element.49, f32[2,16,64]{2,1,0:T(8,128)S(1)} %get-tuple-element.51, f32[2,64,16]{1,2,0:T(8,128)S(1)} %get-tuple-element.50), kind=kOutput, calls=%fused_computation.42 | convolution fusion | flops 34340864 | bytes 2121728 | tf_op jit(solution)/shard_map/bhqk,bkhd->bhqd/dot_general | solution.py:91
  83.0 9.9 %psum.7 = f32[2,64]{1,0:T(2,128)S(1)} all-reduce(f32[2,64]{1,0:T(2,128)S(1)} %get-tuple-element.74), channel_id=1, replica_groups=mesh['ctx'=8,'dp'=4] {'dp'}, use_global_device_ids=true, to_apply=%region_20.21 | all-reduce | flops 128 | bytes 1024 | tf_op jit(solution)/shard_map/psum | solution.py:116
  (78 shorter events, 19.4 us)
Async XLA Ops:
  1.0 13.0 %collective-permute-start.1 = (bf16[6,3,2048]{2,0,1:T(8,128)(2,1)S(1)}, bf16[6,3,2048]{2,0,1:T(8,128)(2,1)S(1)}, u32[]{:S(2)}, u32[]{:S(2)}) collective-permute-start(bf16[6,3,2048]{2,0,1:T(8,128)(2,1)S(1)} %get-tuple-element.28), channel_id=1, source_target_pairs={{4,0},{8,4},{12,8},{16,12},{20,16},{24,20},{28,24},{5,1},{9,5},{13... | collective-permute-start | bytes 221192 | tf_op jit(solution)/shard_map/ppermute | solution.py:18
  2.9 12.2 %collective-permute-start = (bf16[6,3,2048]{2,0,1:T(8,128)(2,1)S(1)}, bf16[6,3,2048]{2,0,1:T(8,128)(2,1)S(1)}, u32[]{:S(2)}, u32[]{:S(2)}) collective-permute-start(bf16[6,3,2048]{2,0,1:T(8,128)(2,1)S(1)} %get-tuple-element.29), channel_id=1, source_target_pairs={{0,4},{4,8},{8,12},{12,16},{16,20},{20,24},{24,28},{1,5},{5,9},{9,... | collective-permute-start | bytes 221192 | tf_op jit(solution)/shard_map/ppermute | solution.py:15
  8.1 1.5 %copy-start = (f32[3,7,128]{2,1,0:T(8,128)S(1)}, f32[3,7,128]{2,1,0:T(8,128)}, u32[]{:S(2)}) copy-start(f32[3,7,128]{2,1,0:T(8,128)} %param.5) | copy-start | bytes 32260
  18.6 9.8 %collective-permute-start.3 = (bf16[64,2,2048]{2,0,1:T(8,128)(2,1)S(1)}, bf16[64,2,2048]{2,0,1:T(8,128)(2,1)S(1)}, u32[]{:S(2)}, u32[]{:S(2)}) collective-permute-start(bf16[64,2,2048]{2,0,1:T(8,128)(2,1)S(1)} %get-tuple-element.23), channel_id=1, source_target_pairs={{4,0},{8,4},{12,8},{16,12},{20,16},{24,20},{28,24},{5,1},{9,5},{13... | collective-permute-start | bytes 1572872 | tf_op jit(solution)/shard_map/ppermute | solution.py:26
  22.1 10.5 %collective-permute-start.2 = (bf16[64,2,2048]{2,0,1:T(8,128)(2,1)S(1)}, bf16[64,2,2048]{2,0,1:T(8,128)(2,1)S(1)}, u32[]{:S(2)}, u32[]{:S(2)}) collective-permute-start(bf16[64,2,2048]{2,0,1:T(8,128)(2,1)S(1)} %get-tuple-element.24), channel_id=1, source_target_pairs={{0,4},{4,8},{8,12},{12,16},{16,20},{20,24},{24,28},{1,5},{5,9},{9,... | collective-permute-start | bytes 1572872 | tf_op jit(solution)/shard_map/ppermute | solution.py:26
  28.5 10.8 %collective-permute-start.5 = (bf16[64,2,2048]{2,0,1:T(8,128)(2,1)S(1)}, bf16[64,2,2048]{2,0,1:T(8,128)(2,1)S(1)}, u32[]{:S(2)}, u32[]{:S(2)}) collective-permute-start(bf16[64,2,2048]{2,0,1:T(8,128)(2,1)S(1)} %broadcast_select_fusion.3), channel_id=1, source_target_pairs={{4,0},{8,4},{12,8},{16,12},{20,16},{24,20},{28,24},{5,1},{9,5},{13... | collective-permute-start | bytes 1572872 | tf_op jit(solution)/shard_map/ppermute | solution.py:26
  32.8 10.6 %collective-permute-start.4 = (bf16[64,2,2048]{2,0,1:T(8,128)(2,1)S(1)}, bf16[64,2,2048]{2,0,1:T(8,128)(2,1)S(1)}, u32[]{:S(2)}, u32[]{:S(2)}) collective-permute-start(bf16[64,2,2048]{2,0,1:T(8,128)(2,1)S(1)} %collective-permute-done.2), channel_id=1, source_target_pairs={{0,4},{4,8},{8,12},{12,16},{16,20},{20,24},{24,28},{1,5},{5,9},{9,... | collective-permute-start | bytes 1572872 | tf_op jit(solution)/shard_map/ppermute | solution.py:26
  39.3 10.8 %collective-permute-start.7 = (bf16[64,2,2048]{2,0,1:T(8,128)(2,1)S(1)}, bf16[64,2,2048]{2,0,1:T(8,128)(2,1)S(1)}, u32[]{:S(2)}, u32[]{:S(2)}) collective-permute-start(bf16[64,2,2048]{2,0,1:T(8,128)(2,1)S(1)} %broadcast_select_fusion.2), channel_id=1, source_target_pairs={{4,0},{8,4},{12,8},{16,12},{20,16},{24,20},{28,24},{5,1},{9,5},{13... | collective-permute-start | bytes 1572872 | tf_op jit(solution)/shard_map/ppermute | solution.py:26
  43.7 10.6 %collective-permute-start.6 = (bf16[64,2,2048]{2,0,1:T(8,128)(2,1)S(1)}, bf16[64,2,2048]{2,0,1:T(8,128)(2,1)S(1)}, u32[]{:S(2)}, u32[]{:S(2)}) collective-permute-start(bf16[64,2,2048]{2,0,1:T(8,128)(2,1)S(1)} %collective-permute-done.4), channel_id=1, source_target_pairs={{0,4},{4,8},{8,12},{12,16},{16,20},{20,24},{24,28},{1,5},{5,9},{9,... | collective-permute-start | bytes 1572872 | tf_op jit(solution)/shard_map/ppermute | solution.py:26
  50.2 10.8 %collective-permute-start.9 = (bf16[64,2,2048]{2,0,1:T(8,128)(2,1)S(1)}, bf16[64,2,2048]{2,0,1:T(8,128)(2,1)S(1)}, u32[]{:S(2)}, u32[]{:S(2)}) collective-permute-start(bf16[64,2,2048]{2,0,1:T(8,128)(2,1)S(1)} %broadcast_select_fusion.1), channel_id=1, source_target_pairs={{4,0},{8,4},{12,8},{16,12},{20,16},{24,20},{28,24},{5,1},{9,5},{13... | collective-permute-start | bytes 1572872 | tf_op jit(solution)/shard_map/ppermute | solution.py:26
  54.5 10.6 %collective-permute-start.8 = (bf16[64,2,2048]{2,0,1:T(8,128)(2,1)S(1)}, bf16[64,2,2048]{2,0,1:T(8,128)(2,1)S(1)}, u32[]{:S(2)}, u32[]{:S(2)}) collective-permute-start(bf16[64,2,2048]{2,0,1:T(8,128)(2,1)S(1)} %collective-permute-done.6), channel_id=1, source_target_pairs={{0,4},{4,8},{8,12},{12,16},{16,20},{20,24},{24,28},{1,5},{5,9},{9,... | collective-permute-start | bytes 1572872 | tf_op jit(solution)/shard_map/ppermute | solution.py:26
  61.0 10.8 %collective-permute-start.11 = (bf16[64,2,2048]{2,0,1:T(8,128)(2,1)S(1)}, bf16[64,2,2048]{2,0,1:T(8,128)(2,1)S(1)}, u32[]{:S(2)}, u32[]{:S(2)}) collective-permute-start(bf16[64,2,2048]{2,0,1:T(8,128)(2,1)S(1)} %broadcast_select_fusion), channel_id=1, source_target_pairs={{4,0},{8,4},{12,8},{16,12},{20,16},{24,20},{28,24},{5,1},{9,5},{13... | collective-permute-start | bytes 1572872 | tf_op jit(solution)/shard_map/ppermute | solution.py:26
  65.4 10.5 %collective-permute-start.10 = (bf16[64,2,2048]{2,0,1:T(8,128)(2,1)S(1)}, bf16[64,2,2048]{2,0,1:T(8,128)(2,1)S(1)}, u32[]{:S(2)}, u32[]{:S(2)}) collective-permute-start(bf16[64,2,2048]{2,0,1:T(8,128)(2,1)S(1)} %collective-permute-done.8), channel_id=1, source_target_pairs={{0,4},{4,8},{8,12},{12,16},{16,20},{20,24},{24,28},{1,5},{5,9},{9,... | collective-permute-start | bytes 1572872 | tf_op jit(solution)/shard_map/ppermute | solution.py:26
  93.5 0.7 copy-start.1
where the time goes:
time: 95.7 us; the launch traced here: 95.1 us
  starting transfers between devices  33.7 us (35%)
  waiting for transfers between devices  23.5 us (25%)
  other arithmetic  13.2 us (14%)
  blocking collectives  9.91 us (10%)
  matrix products  7.47 us (8%)
  local copies, waits for them, and re-layouts  6.84 us (7%)
    ppermute x10, starting transfers between devices, shifted(): return lax.ppermute(block, axis, route)  29.4 us
    ppermute x10, waiting for transfers between devices, shifted(): return lax.ppermute(block, axis, route)  23.5 us
    psum x1, blocking collectives, local(): total_sq = lax.psum(squares, 'dp')  9.91 us
    dot_general x6, matrix products, tile(): jnp.einsum('bhqk,bkhd->bhqd', weights, values_blk, preferred_element_type...  4.86 us
    convert_element_type x1, other arithmetic, local(): conv = summed.astype(jnp.bfloat16)  3.12 us
    dot_general x6, matrix products, tile(): jnp.einsum('bqhd,bkhd->bhqk', queries, keys_blk, preferred_element_type=j...  2.61 us
    ppermute x1, starting transfers between devices, extended(): lax.ppermute(lax.slice_in_dim(block, block.shape[dim] - width, None, axis...  2.41 us
    unnamed x21, local copies, waits for them, and re-layouts  2.1 us
  transfers between devices with their start and end apart: 12, of which 6 were waited for; matrix products, arithmetic and copies ran while one was open for 15% of the time, Pallas kernels for 0%

commit v1 on v0

v1 whole, which is shorter than its diff:
```python
import functools

import jax
import jax.numpy as jnp
from jax import lax
from jax.experimental import pallas as pl
from jax.experimental.pallas import tpu as pltpu
from jax.sharding import PartitionSpec as P

HEAD_DIM = 128
REACH = 5
RIM = 8
HEAD_ROWS = 16
PAIRS = (REACH + 1) // 2
MESH = pl.DeviceIdType.MESH


def kernel(
    n_ctx,
    n_dp,
    x_ref,
    f_ref,
    gain_ref,
    docs_ref,
    out_ref,
    xs,
    xf,
    fw,
    halo,
    qb,
    kv,
    run_max,
    run_total,
    acc,
    squares,
    inv_norm,
    sq_own,
    sq_peer,
    starts,
    load_sem,
    halo_send,
    halo_recv,
    kv_send,
    kv_recv,
    sq_send,
    sq_recv,
):
    rows = xs.shape[2]
    width = xs.shape[3]
    groups = kv.shape[1]
    group_width = kv.shape[4]
    group_heads = group_width // HEAD_DIM
    taps = f_ref.shape[1]
    place = lax.axis_index("ctx")
    lane = lax.axis_index("dp")
    right = lax.rem(place + 1, n_ctx)
    left = lax.rem(place + n_ctx - 1, n_ctx)
    has_left = place > 0
    has_right = place < n_ctx - 1
    is_last = place == n_ctx - 1

    load_kv = [
        pltpu.make_async_copy(x_ref.at[b, pl.ds(1, 2)], xs.at[b, pl.ds(1, 2)], load_sem.at[b])
        for b in range(2)
    ]
    load_q = [
        pltpu.make_async_copy(x_ref.at[b, 0], xs.at[b, 0], load_sem.at[2 + b]) for b in range(2)
    ]
    for copy in load_kv + load_q:
        copy.start()

    barrier = pltpu.get_barrier_semaphore()

    @pl.when(has_left)
    def _():
        pl.semaphore_signal(barrier, inc=1, device_id={"ctx": left}, device_id_type=MESH)

    @pl.when(has_right)
    def _():
        pl.semaphore_signal(barrier, inc=1, device_id={"ctx": right}, device_id_type=MESH)

    for step in range(1, n_dp):
        peer = lax.rem(lane + step, n_dp)
        pl.semaphore_signal(barrier, inc=1, device_id={"dp": peer}, device_id_type=MESH)

    def rim(b, source, target):
        return pltpu.make_async_remote_copy(
            src_ref=x_ref.at[source, :, pl.ds(rows - RIM, RIM), :],
            dst_ref=halo.at[b],
            send_sem=halo_send.at[b],
            recv_sem=halo_recv.at[b],
            device_id={"ctx": target},
            device_id_type=MESH,
        )

    rim_lower = rim(0, 0, right)
    rim_upper = rim(1, 1, left)
    rim_fold = pltpu.make_async_copy(
        x_ref.at[0, :, pl.ds(rows - RIM, RIM), :], halo.at[1], halo_recv.at[1]
    )
    pl.semaphore_wait(barrier, n_dp - 1 + has_left.astype(jnp.int32) + has_right.astype(jnp.int32))

    @pl.when(has_right)
    def _():
        rim_lower.start()

    @pl.when(has_left)
    def _():
        rim_upper.start()

    @pl.when(is_last)
    def _():
        rim_fold.start()

    spread_shape = (f_ref.shape[2], HEAD_DIM)
    spread_row = lax.broadcasted_iota(jnp.int32, spread_shape, 0)
    spread_col = lax.broadcasted_iota(jnp.int32, spread_shape, 1)
    group_size = width // f_ref.shape[2]
    for m in range(3):
        taps_m = f_ref[m]
        for h in range(width // HEAD_DIM):
            first = h * HEAD_DIM
            hot = (spread_row * group_size <= first + spread_col) & (
                first + spread_col < (spread_row + 1) * group_size
            )
            fw[m, pl.ds(0, taps), pl.ds(first, HEAD_DIM)] = jnp.dot(
                taps_m,
                jnp.where(hot, 1.0, 0.0).astype(jnp.float32),
                precision=lax.Precision.HIGHEST,
                preferred_element_type=jnp.float32,
            )

    for d in range(1, REACH + 1):

        @pl.when(place < d)
        def _():
            def clear(g, carry):
                kv[0, g, :, pl.ds(d * rows, rows), :] = jnp.zeros(
                    (2, rows, group_width), jnp.bfloat16
                )
                return carry

            lax.fori_loop(0, groups, clear, 0)

    @pl.when(place == 0)
    def _():
        halo[0] = jnp.zeros(halo.shape[1:], jnp.bfloat16)

    offsets = lax.broadcasted_iota(jnp.int32, (rows, HEAD_DIM), 0)
    block_start = [place * rows, (2 * n_ctx - 1 - place) * rows]
    for b in range(2):
        positions = block_start[b] + offsets

        def advance(k, carry):
            begin, end = carry
            end = end + docs_ref[k]
            return jnp.where(positions >= end, end, begin), end

        begin, _ = lax.fori_loop(
            0, docs_ref.shape[0], advance, (jnp.zeros_like(positions), jnp.int32(0))
        )
        starts[b] = begin

    def convolved(b, m, lanes, first, count):
        total = None
        for s in range(taps):
            term = fw[m, pl.ds(s, 1), lanes] * xf[b, m, pl.ds(first + RIM - taps + 1 + s, count), lanes]
            total = term if total is None else total + term
        return total.astype(jnp.bfloat16)

    def channel(g, hl):
        return pl.ds(pl.multiple_of(g * group_width + hl * HEAD_DIM, HEAD_DIM), HEAD_DIM)

    def inner(hl):
        return pl.ds(hl * HEAD_DIM, HEAD_DIM)

    for copy in load_kv:
        copy.wait()

    def body_rows(i, carry):
        b, g = lax.div(i, groups), lax.rem(i, groups)
        for m in (1, 2):
            for hl in range(group_heads):
                lanes = channel(g, hl)
                xf[b, m, pl.ds(RIM, rows), lanes] = xs[b, m, :, lanes].astype(jnp.float32)
            for hl in range(group_heads):
                kv[b, g, m - 1, pl.ds(HEAD_ROWS, rows - HEAD_ROWS), inner(hl)] = convolved(
                    b, m, channel(g, hl), HEAD_ROWS, rows - HEAD_ROWS
                )
        return carry

    lax.fori_loop(0, 2 * groups, body_rows, 0)

    @pl.when(has_left)
    def _():
        rim_lower.wait_recv()

    @pl.when(has_right)
    def _():
        rim_upper.wait_recv()

    @pl.when(is_last)
    def _():
        rim_fold.wait()

    def slot(b, g, d):
        return kv.at[b, g, :, pl.ds(d * rows, rows), :]

    def moved(b, g, d, target):
        return pltpu.make_async_remote_copy(
            src_ref=slot(b, g, d - 1),
            dst_ref=slot(b, g, d),
            send_sem=kv_send.at[b, d - 1, g],
            recv_sem=kv_recv.at[b, d - 1, g],
            device_id={"ctx": target},
            device_id_type=MESH,
        )

    def folded(g, d):
        return pltpu.make_async_copy(slot(0, g, d - 1), slot(1, g, d), kv_recv.at[1, d - 1, g])

    def lower_sends(d):
        return has_right & (place + 1 >= d)

    def launch(g, d):
        @pl.when(has_left)
        def _():
            moved(1, g, d, left).start()

        @pl.when(lower_sends(d))
        def _():
            moved(0, g, d, right).start()

        @pl.when(is_last)
        def _():
            folded(g, d).start()

    def arrive(g, d):
        @pl.when(place >= d)
        def _():
            moved(0, g, d, right).wait_recv()

        @pl.when(has_right)
        def _():
            moved(1, g, d, left).wait_recv()

        @pl.when(is_last)
        def _():
            folded(g, d).wait()

    def first_rows(g, carry):
        for b in range(2):
            for m in (1, 2):
                for hl in range(group_heads):
                    lanes = channel(g, hl)
                    xf[b, m, pl.ds(0, RIM), lanes] = halo[b, m, :, lanes].astype(jnp.float32)
                    kv[b, g, m - 1, pl.ds(0, HEAD_ROWS), inner(hl)] = convolved(
                        b, m, lanes, 0, HEAD_ROWS
                    )
        launch(g, 1)
        return carry

    lax.fori_loop(0, groups, first_rows, 0)

    for copy in load_q:
        copy.wait()

    def query_rows(i, carry):
        b, g = lax.div(i, groups), lax.rem(i, groups)
        for hl in range(group_heads):
            lanes = channel(g, hl)
            xf[b, 0, pl.ds(0, RIM), lanes] = halo[b, 0, :, lanes].astype(jnp.float32)
            xf[b, 0, pl.ds(RIM, rows), lanes] = xs[b, 0, :, lanes].astype(jnp.float32)
        for hl in range(group_heads):
            qb[b, g, :, inner(hl)] = convolved(b, 0, channel(g, hl), 0, rows)
        return carry

    lax.fori_loop(0, 2 * groups, query_rows, 0)

    key_lane = lax.broadcasted_iota(jnp.int32, (rows, HEAD_DIM), 1)
    key_offset = jnp.where(key_lane >= rows, key_lane - 2 * rows, key_lane)
    span = 2 * rows

    def attend(pair, b, g):
        block = place * rows if b == 0 else (2 * n_ctx - 1 - place) * rows
        key_pos = key_offset + (block - pair * span)
        allowed = (key_pos >= starts[b]) & (key_pos <= block + offsets)
        for hl in range(group_heads):
            lanes = inner(hl)
            query = qb[b, g, :, lanes]
            key = kv[b, g, 0, pl.ds(pair * span, span), lanes]
            value = kv[b, g, 1, pl.ds(pair * span, span), lanes]
            scores = lax.dot_general(
                query, key, (((1,), (1,)), ((), ())), preferred_element_type=jnp.float32
            ) * HEAD_DIM ** (-0.5)
            scores = jnp.where(allowed, scores, -1e30)
            top = jnp.max(scores, axis=1, keepdims=True)
            if pair > 0:
                before = run_max[b, g, hl]
                top = jnp.maximum(before, top)
            expo = jnp.exp(scores - top)
            total = jnp.sum(expo, axis=1, keepdims=True)
            update = jnp.dot(
                expo.astype(jnp.bfloat16), value, preferred_element_type=jnp.float32
            )
            if pair > 0:
                rescale = jnp.exp(before - top)
                total = run_total[b, g, hl] * rescale + total
                update = acc[b, g, :, lanes] * rescale + update
            if pair < PAIRS - 1:
                run_max[b, g, hl] = jnp.broadcast_to(top, (rows, HEAD_DIM))
                run_total[b, g, hl] = jnp.broadcast_to(total, (rows, HEAD_DIM))
                acc[b, g, :, lanes] = update
            else:
                attended = update / total
                acc[b, g, :, lanes] = attended
                squares[pl.ds(b * rows, rows), :] += attended * attended

    squares[...] = jnp.zeros_like(squares)
    for d in range(1, REACH):

        def relay(g, carry):
            arrive(g, d)
            launch(g, d + 1)
            return carry

        lax.fori_loop(0, groups, relay, 0)
        if d % 2 == 1:

            def work(g, carry):
                for b in range(2):
                    attend(d // 2, b, g)
                return carry

            lax.fori_loop(0, groups, work, 0)

    def finish(g, carry):
        arrive(g, REACH)
        for b in range(2):
            attend(PAIRS - 1, b, g)
        return carry

    lax.fori_loop(0, groups, finish, 0)

    row = jnp.sum(jnp.transpose(squares[...]), axis=0, keepdims=True)
    sq_own[...] = jnp.broadcast_to(row, sq_own.shape)
    shares = []
    for step in range(1, n_dp):
        share = pltpu.make_async_remote_copy(
            src_ref=sq_own,
            dst_ref=sq_peer.at[step - 1],
            send_sem=sq_send.at[step - 1],
            recv_sem=sq_recv.at[step - 1],
            device_id={"dp": lax.rem(lane + step, n_dp)},
            device_id_type=MESH,
        )
        share.start()
        shares.append(share)

    @pl.when(has_right)
    def _():
        rim_lower.wait_send()

    @pl.when(has_left)
    def _():
        rim_upper.wait_send()

    for d in range(1, REACH + 1):

        def drain(g, carry):
            @pl.when(has_left)
            def _():
                moved(1, g, d, left).wait_send()

            @pl.when(lower_sends(d))
            def _():
                moved(0, g, d, right).wait_send()

            return carry

        lax.fori_loop(0, groups, drain, 0)

    whole = sq_own[...]
    for step in range(1, n_dp):
        shares[step - 1].wait()
        whole = whole + sq_peer[step - 1]
    inverse = lax.rsqrt(whole / (width * n_dp) + 1e-06)
    inv_norm[...] = jnp.transpose(jnp.broadcast_to(inverse[0:1], inv_norm.shape))

    def norm(g, carry):
        for b in range(2):
            factor = inv_norm[pl.ds(b * rows, rows), :]
            for hl in range(group_heads):
                lanes = channel(g, hl)
                out_ref[b, :, lanes] = (
                    acc[b, g, :, inner(hl)] * factor * gain_ref[:, lanes]
                ).astype(jnp.bfloat16)
        return carry

    lax.fori_loop(0, groups, norm, 0)


def local(n_ctx, n_dp, projected, filters, gain, doc_lengths):
    blocks = jnp.transpose(projected[0], (0, 2, 1, 3))
    rows, width = blocks.shape[2], blocks.shape[3]
    group_width = min(width, 4 * HEAD_DIM)
    groups = width // group_width
    group_heads = group_width // HEAD_DIM
    vmem = pl.BlockSpec(memory_space=pltpu.VMEM)
    out = pl.pallas_call(
        functools.partial(kernel, n_ctx, n_dp),
        out_shape=jax.ShapeDtypeStruct((2, rows, width), jnp.bfloat16),
        in_specs=[
            pl.BlockSpec(memory_space=pl.ANY),
            vmem,
            vmem,
            pl.BlockSpec(memory_space=pltpu.SMEM),
        ],
        out_specs=vmem,
        scratch_shapes=[
            pltpu.VMEM((2, 3, rows, width), jnp.bfloat16),
            pltpu.VMEM((2, 3, RIM + rows, width), jnp.float32),
            pltpu.VMEM((3, 8, width), jnp.float32),
            pltpu.VMEM((2, 3, RIM, width), jnp.bfloat16),
            pltpu.VMEM((2, groups, rows, group_width), jnp.bfloat16),
            pltpu.VMEM((2, groups, 2, (REACH + 1) * rows, group_width), jnp.bfloat16),
            pltpu.VMEM((2, groups, group_heads, rows, HEAD_DIM), jnp.float32),
            pltpu.VMEM((2, groups, group_heads, rows, HEAD_DIM), jnp.float32),
            pltpu.VMEM((2, groups, rows, group_width), jnp.float32),
            pltpu.VMEM((2 * rows, HEAD_DIM), jnp.float32),
            pltpu.VMEM((2 * rows, HEAD_DIM), jnp.float32),
            pltpu.VMEM((8, 2 * rows), jnp.float32),
            pltpu.VMEM((n_dp - 1, 8, 2 * rows), jnp.float32),
            pltpu.VMEM((2, rows, HEAD_DIM), jnp.int32),
            pltpu.SemaphoreType.DMA((4,)),
            pltpu.SemaphoreType.DMA((2,)),
            pltpu.SemaphoreType.DMA((2,)),
            pltpu.SemaphoreType.DMA((2, REACH, groups)),
            pltpu.SemaphoreType.DMA((2, REACH, groups)),
            pltpu.SemaphoreType.DMA((n_dp - 1,)),
            pltpu.SemaphoreType.DMA((n_dp - 1,)),
        ],
        compiler_params=pltpu.CompilerParams(
            collective_id=0, has_side_effects=True, vmem_limit_bytes=48 * 1024 * 1024
        ),
    )(blocks, filters, gain[None, :], doc_lengths)
    return out[None]


def solution(mesh):
    in_specs = (P("ctx", None, None, None, "dp"), P(None, None, "dp"), P("dp"), P())
    out_specs = P("ctx", None, None, "dp")
    return jax.shard_map(
        functools.partial(local, mesh.shape["ctx"], mesh.shape["dp"]),
        mesh=mesh,
        in_specs=in_specs,
        out_specs=out_specs,
        check_vma=False,
    )
```

time: 95.7 us -> 59.8 us (0.62)
  Pallas kernels: 0 us -> 55.2 us
  starting transfers between devices: 33.7 us -> 0 us
  waiting for transfers between devices: 23.5 us -> 0 us
  other arithmetic: 13.2 us -> 0 us
  blocking collectives: 9.91 us -> 0 us
  matrix products: 7.47 us -> 0 us
  local copies, waits for them, and re-layouts: 6.84 us -> 4.26 us
    pallas_call x0 -> x1, Pallas kernels: none -> 55.2 us  [local(): pl.pallas_call(functools.partial(kernel, n_ctx, n_dp), out_shape=jax.Shap...]
    ppermute x12 -> x0, starting transfers between devices: 33.7 us -> none  [the longest x10 29.4 us: shifted(): return lax.ppermute(block, axis, route)]
    ppermute x12 -> x0, waiting for transfers between devices: 23.5 us -> none  [the longest x10 23.5 us: shifted(): return lax.ppermute(block, axis, route)]
    psum x1 -> x0, blocking collectives: 9.91 us -> none  [local(): total_sq = lax.psum(squares, 'dp')]
    dot_general x12 -> x0, matrix products: 7.47 us -> none  [the longest x6 4.86 us: tile(): jnp.einsum('bhqk,bkhd->bhqd', weights, values_blk, preferred_element_type...]
    convert_element_type x2 -> x0, other arithmetic: 4.06 us -> none  [the longest x1 3.12 us: local(): conv = summed.astype(jnp.bfloat16)]
    squeeze x3 -> x0, local copies, waits for them, and re-layouts: 2.54 us -> none  [the longest x1 1.48 us: local(): blocks[1]]
    unnamed x21 -> x9, local copies, waits for them, and re-layouts: 2.1 us -> 4.26 us
  transfers between devices with their start and end apart: 12 -> 0, of which waited for: 6 -> 0; matrix products, arithmetic and copies ran while one was open for 15% -> 0% of each run, Pallas kernels for 0% -> 0%
where the time goes in v1:
time: 59.8 us; the launch traced here: 59.5 us
  Pallas kernels  55.2 us (92%)
  local copies, waits for them, and re-layouts  4.26 us (7%)
    pallas_call x1, Pallas kernels, local(): pl.pallas_call(functools.partial(kernel, n_ctx, n_dp), out_shape=jax.Shap...  55.2 us
    unnamed x9, local copies, waits for them, and re-layouts  4.26 us

profile of v1, /device:TPU:24, one launch (start us, length us, event | category | flops | bytes accessed | tf_op | source)
XLA Modules:
  0.0 59.5 jit_solution(7380336779317193485)
XLA Ops:
  0.0 0.0 copy-start
  0.0 1.4 %copy-done = bf16[1,2,64,3,2048]{4,2,3,1,0:T(8,128)(2,1)S(1)} copy-done((bf16[1,2,64,3,2048]{4,2,3,1,0:T(8,128)(2,1)S(1)}, bf16[1,2,64,3,2048]{4,2,3,1,0:T(8,128)(2,1)}, u32[]{:S(2)}) %copy-start) | copy-done | bytes 1572888
  1.4 0.0 copy-start.1
  1.4 0.7 %copy-done.1 = f32[3,7,128]{2,1,0:T(8,128)S(1)} copy-done((f32[3,7,128]{2,1,0:T(8,128)S(1)}, f32[3,7,128]{2,1,0:T(8,128)}, u32[]{:S(2)}) %copy-start.1) | copy-done | bytes 10776
  2.1 0.0 copy-start.2
  2.1 0.7 %copy-done.2 = f32[2048]{0:T(1024)S(1)} copy-done((f32[2048]{0:T(1024)S(1)}, f32[2048]{0:T(1024)}, u32[]{:S(2)}) %copy-start.2) | copy-done | bytes 8216
  2.8 0.0 copy-start.3
  2.8 0.7 %copy-done.3 = s32[4]{0:T(128)S(1)} copy-done((s32[4]{0:T(128)S(1)}, s32[4]{0:T(128)}, u32[]{:S(2)}) %copy-start.3) | copy-done | bytes 40
  3.5 55.2 %shard_map.46 = bf16[2,64,2048]{2,1,0:T(8,128)(2,1)S(1)} custom-call(bf16[2,3,64,2048]{3,2,1,0:T(8,128)(2,1)S(1)} %bitcast.6, f32[3,7,128]{2,1,0:T(8,128)S(1)} %copy-done.1, f32[1,2048]{1,0:T(1,128)S(1)} %bitcast.7, s32[4]{0:T(128)S(1)} %copy-done.3), custom_call_target="tpu_custom_call" | custom-call | tf_op jit(solution)/shard_map/pallas_call | solution.py:410
  58.7 0.8 %copy.6 = bf16[1,2,64,2048]{3,2,1,0:T(8,128)(2,1)} copy(bf16[1,2,64,2048]{3,2,1,0:T(8,128)(2,1)S(1)} %bitcast.5) | data formatting | bytes 1048576
Async XLA Ops:
  0.0 1.4 %copy-start = (bf16[1,2,64,3,2048]{4,2,3,1,0:T(8,128)(2,1)S(1)}, bf16[1,2,64,3,2048]{4,2,3,1,0:T(8,128)(2,1)}, u32[]{:S(2)}) copy-start(bf16[1,2,64,3,2048]{4,2,3,1,0:T(8,128)(2,1)} %param.4) | copy-start | bytes 4718596
  1.4 0.7 %copy-start.1 = (f32[3,7,128]{2,1,0:T(8,128)S(1)}, f32[3,7,128]{2,1,0:T(8,128)}, u32[]{:S(2)}) copy-start(f32[3,7,128]{2,1,0:T(8,128)} %f_ref.1) | copy-start | bytes 32260
  2.1 0.7 %copy-start.2 = (f32[2048]{0:T(1024)S(1)}, f32[2048]{0:T(1024)}, u32[]{:S(2)}) copy-start(f32[2048]{0:T(1024)} %param.6) | copy-start | bytes 24580
  2.8 0.7 %copy-start.3 = (s32[4]{0:T(128)S(1)}, s32[4]{0:T(128)}, u32[]{:S(2)}) copy-start(s32[4]{0:T(128)} %docs_ref.1) | copy-start | bytes 52

commit v2 on v1

--- a/solution.py
+++ b/solution.py
@@ -1,4 +1,5 @@
 import functools
+import math
 
 import jax
 import jax.numpy as jnp
@@ -12,6 +13,7 @@
 RIM = 8
 HEAD_ROWS = 16
 PAIRS = (REACH + 1) // 2
+LOG2_SCALE = HEAD_DIM ** (-0.5) * math.log2(math.e)
 MESH = pl.DeviceIdType.MESH
 
 
@@ -19,10 +21,14 @@
     n_ctx,
     n_dp,
     x_ref,
+    f_hbm,
+    gain_hbm,
+    docs_hbm,
+    out_ref,
     f_ref,
     gain_ref,
     docs_ref,
-    out_ref,
+    parts,
     xs,
     xf,
     fw,
@@ -66,7 +72,12 @@
     load_q = [
         pltpu.make_async_copy(x_ref.at[b, 0], xs.at[b, 0], load_sem.at[2 + b]) for b in range(2)
     ]
-    for copy in load_kv + load_q:
+    load_small = [
+        pltpu.make_async_copy(f_hbm, f_ref, load_sem.at[4]),
+        pltpu.make_async_copy(docs_hbm, docs_ref, load_sem.at[5]),
+        pltpu.make_async_copy(gain_hbm, gain_ref, load_sem.at[6]),
+    ]
+    for copy in load_small + load_kv + load_q:
         copy.start()
 
     barrier = pltpu.get_barrier_semaphore()
@@ -98,68 +109,45 @@
     rim_fold = pltpu.make_async_copy(
         x_ref.at[0, :, pl.ds(rows - RIM, RIM), :], halo.at[1], halo_recv.at[1]
     )
-    pl.semaphore_wait(barrier, n_dp - 1 + has_left.astype(jnp.int32) + has_right.astype(jnp.int32))
-
-    @pl.when(has_right)
-    def _():
-        rim_lower.start()
-
-    @pl.when(has_left)
-    def _():
-        rim_upper.start()
-
-    @pl.when(is_last)
-    def _():
-        rim_fold.start()
-
     spread_shape = (f_ref.shape[2], HEAD_DIM)
     spread_row = lax.broadcasted_iota(jnp.int32, spread_shape, 0)
     spread_col = lax.broadcasted_iota(jnp.int32, spread_shape, 1)
     group_size = width // f_ref.shape[2]
+    parts[...] = jnp.zeros_like(parts)
+    load_small[0].wait()
     for m in range(3):
-        taps_m = f_ref[m]
-        for h in range(width // HEAD_DIM):
-            first = h * HEAD_DIM
-            hot = (spread_row * group_size <= first + spread_col) & (
-                first + spread_col < (spread_row + 1) * group_size
-            )
-            fw[m, pl.ds(0, taps), pl.ds(first, HEAD_DIM)] = jnp.dot(
-                taps_m,
-                jnp.where(hot, 1.0, 0.0).astype(jnp.float32),
-                precision=lax.Precision.HIGHEST,
-                preferred_element_type=jnp.float32,
-            )
-
-    for d in range(1, REACH + 1):
-
-        @pl.when(place < d)
-        def _():
-            def clear(g, carry):
-                kv[0, g, :, pl.ds(d * rows, rows), :] = jnp.zeros(
-                    (2, rows, group_width), jnp.bfloat16
-                )
-                return carry
-
-            lax.fori_loop(0, groups, clear, 0)
-
-    @pl.when(place == 0)
-    def _():
-        halo[0] = jnp.zeros(halo.shape[1:], jnp.bfloat16)
-
-    offsets = lax.broadcasted_iota(jnp.int32, (rows, HEAD_DIM), 0)
-    block_start = [place * rows, (2 * n_ctx - 1 - place) * rows]
-    for b in range(2):
-        positions = block_start[b] + offsets
-
-        def advance(k, carry):
-            begin, end = carry
-            end = end + docs_ref[k]
-            return jnp.where(positions >= end, end, begin), end
-
-        begin, _ = lax.fori_loop(
-            0, docs_ref.shape[0], advance, (jnp.zeros_like(positions), jnp.int32(0))
+        left_over = f_ref[m]
+        for part in range(3):
+            piece = left_over.astype(jnp.bfloat16).astype(jnp.float32)
+            parts[3 * part + m, pl.ds(0, taps), :] = piece
+            left_over = left_over - piece
+    split = parts[...].reshape(72, f_ref.shape[2]).astype(jnp.bfloat16)
+    for h in range(width // HEAD_DIM):
+        first = h * HEAD_DIM
+        hot = (spread_row * group_size <= first + spread_col) & (
+            first + spread_col < (spread_row + 1) * group_size
         )
-        starts[b] = begin
+        spread = jnp.dot(
+            split,
+            jnp.where(hot, 1.0, 0.0).astype(jnp.bfloat16),
+            preferred_element_type=jnp.float32,
+        ).reshape(9, 8, HEAD_DIM)
+        for m in range(3):
+            fw[m, :, pl.ds(first, HEAD_DIM)] = (spread[m] + spread[3 + m]) + spread[6 + m]
+
+    pl.semaphore_wait(barrier, n_dp - 1 + has_left.astype(jnp.int32) + has_right.astype(jnp.int32))
+
+    @pl.when(has_right)
+    def _():
+        rim_lower.start()
+
+    @pl.when(has_left)
+    def _():
+        rim_upper.start()
+
+    @pl.when(is_last)
+    def _():
+        rim_fold.start()
 
     def convolved(b, m, lanes, first, count):
         total = None
@@ -174,42 +162,13 @@
     def inner(hl):
         return pl.ds(hl * HEAD_DIM, HEAD_DIM)
 
-    for copy in load_kv:
-        copy.wait()
-
-    def body_rows(i, carry):
-        b, g = lax.div(i, groups), lax.rem(i, groups)
-        for m in (1, 2):
-            for hl in range(group_heads):
-                lanes = channel(g, hl)
-                xf[b, m, pl.ds(RIM, rows), lanes] = xs[b, m, :, lanes].astype(jnp.float32)
-            for hl in range(group_heads):
-                kv[b, g, m - 1, pl.ds(HEAD_ROWS, rows - HEAD_ROWS), inner(hl)] = convolved(
-                    b, m, channel(g, hl), HEAD_ROWS, rows - HEAD_ROWS
-                )
-        return carry
-
-    lax.fori_loop(0, 2 * groups, body_rows, 0)
-
-    @pl.when(has_left)
-    def _():
-        rim_lower.wait_recv()
-
-    @pl.when(has_right)
-    def _():
-        rim_upper.wait_recv()
-
-    @pl.when(is_last)
-    def _():
-        rim_fold.wait()
-
-    def slot(b, g, d):
-        return kv.at[b, g, :, pl.ds(d * rows, rows), :]
-
-    def moved(b, g, d, target):
+    def slot(b, g, d, first=0, count=rows):
+        return kv.at[b, g, :, pl.ds(d * rows + first, count), :]
+
+    def moved(b, g, d, target, first=0, count=rows):
         return pltpu.make_async_remote_copy(
-            src_ref=slot(b, g, d - 1),
-            dst_ref=slot(b, g, d),
+            src_ref=slot(b, g, d - 1, first, count),
+            dst_ref=slot(b, g, d, first, count),
             send_sem=kv_send.at[b, d - 1, g],
             recv_sem=kv_recv.at[b, d - 1, g],
             device_id={"ctx": target},
@@ -222,18 +181,20 @@
     def lower_sends(d):
         return has_right & (place + 1 >= d)
 
-    def launch(g, d):
+    def launch(g, d, first=0, count=rows):
         @pl.when(has_left)
         def _():
-            moved(1, g, d, left).start()
+            moved(1, g, d, left, first, count).start()
 
         @pl.when(lower_sends(d))
         def _():
-            moved(0, g, d, right).start()
-
-        @pl.when(is_last)
-        def _():
-            folded(g, d).start()
+            moved(0, g, d, right, first, count).start()
+
+        if first == 0:
+
+            @pl.when(is_last)
+            def _():
+                folded(g, d).start()
 
     def arrive(g, d):
         @pl.when(place >= d)
@@ -247,6 +208,40 @@
         @pl.when(is_last)
         def _():
             folded(g, d).wait()
+
+    for copy in load_kv:
+        copy.wait()
+
+    def body_rows(g, carry):
+        for b in range(2):
+            for m in (1, 2):
+                for hl in range(group_heads):
+                    lanes = channel(g, hl)
+                    xf[b, m, pl.ds(RIM, rows), lanes] = xs[b, m, :, lanes].astype(jnp.float32)
+                for hl in range(group_heads):
+                    kv[b, g, m - 1, pl.ds(HEAD_ROWS, rows - HEAD_ROWS), inner(hl)] = convolved(
+                        b, m, channel(g, hl), HEAD_ROWS, rows - HEAD_ROWS
+                    )
+        launch(g, 1, HEAD_ROWS, rows - HEAD_ROWS)
+        return carry
+
+    lax.fori_loop(0, groups, body_rows, 0)
+
+    @pl.when(place == 0)
+    def _():
+        halo[0] = jnp.zeros(halo.shape[1:], jnp.bfloat16)
+
+    @pl.when(has_left)
+    def _():
+        rim_lower.wait_recv()
+
+    @pl.when(has_right)
+    def _():
+        rim_upper.wait_recv()
+
+    @pl.when(is_last)
+    def _():
+        rim_fold.wait()
 
     def first_rows(g, carry):
         for b in range(2):
@@ -257,10 +252,39 @@
                     kv[b, g, m - 1, pl.ds(0, HEAD_ROWS), inner(hl)] = convolved(
                         b, m, lanes, 0, HEAD_ROWS
                     )
-        launch(g, 1)
+        launch(g, 1, 0, HEAD_ROWS)
         return carry
 
     lax.fori_loop(0, groups, first_rows, 0)
+
+    for d in range(1, REACH + 1):
+
+        @pl.when(place < d)
+        def _():
+            def clear(g, carry):
+                kv[0, g, :, pl.ds(d * rows, rows), :] = jnp.zeros(
+                    (2, rows, group_width), jnp.bfloat16
+                )
+                return carry
+
+            lax.fori_loop(0, groups, clear, 0)
+
+    load_small[1].wait()
+
+    offsets = lax.broadcasted_iota(jnp.int32, (rows, HEAD_DIM), 0)
+    block_start = [place * rows, (2 * n_ctx - 1 - place) * rows]
+    for b in range(2):
+        positions = block_start[b] + offsets
+
+        def advance(k, carry):
+            begin, end = carry
+            end = end + docs_ref[k]
+            return jnp.where(positions >= end, end, begin), end
+
+        begin, _ = lax.fori_loop(
+            0, docs_ref.shape[0], advance, (jnp.zeros_like(positions), jnp.int32(0))
+        )
+        starts[b] = begin
 
     for copy in load_q:
         copy.wait()
@@ -285,54 +309,61 @@
         block = place * rows if b == 0 else (2 * n_ctx - 1 - place) * rows
         key_pos = key_offset + (block - pair * span)
         allowed = (key_pos >= starts[b]) & (key_pos <= block + offsets)
-        for hl in range(group_heads):
-            lanes = inner(hl)
-            query = qb[b, g, :, lanes]
-            key = kv[b, g, 0, pl.ds(pair * span, span), lanes]
-            value = kv[b, g, 1, pl.ds(pair * span, span), lanes]
-            scores = lax.dot_general(
-                query, key, (((1,), (1,)), ((), ())), preferred_element_type=jnp.float32
-            ) * HEAD_DIM ** (-0.5)
-            scores = jnp.where(allowed, scores, -1e30)
-            top = jnp.max(scores, axis=1, keepdims=True)
-            if pair > 0:
-                before = run_max[b, g, hl]
-                top = jnp.maximum(before, top)
-            expo = jnp.exp(scores - top)
-            total = jnp.sum(expo, axis=1, keepdims=True)
-            update = jnp.dot(
-                expo.astype(jnp.bfloat16), value, preferred_element_type=jnp.float32
+        heads = range(group_heads)
+        keys = pl.ds(pair * span, span)
+        scores = [
+            lax.dot_general(
+                qb[b, g, :, inner(hl)],
+                kv[b, g, 0, keys, inner(hl)],
+                (((1,), (1,)), ((), ())),
+                preferred_element_type=jnp.float32,
             )
-            if pair > 0:
-                rescale = jnp.exp(before - top)
-                total = run_total[b, g, hl] * rescale + total
-                update = acc[b, g, :, lanes] * rescale + update
-            if pair < PAIRS - 1:
-                run_max[b, g, hl] = jnp.broadcast_to(top, (rows, HEAD_DIM))
-                run_total[b, g, hl] = jnp.broadcast_to(total, (rows, HEAD_DIM))
-                acc[b, g, :, lanes] = update
-            else:
-                attended = update / total
-                acc[b, g, :, lanes] = attended
-                squares[pl.ds(b * rows, rows), :] += attended * attended
+            for hl in heads
+        ]
+        scores = [jnp.where(allowed, score * LOG2_SCALE, -1e30) for score in scores]
+        tops = [jnp.max(score, axis=1, keepdims=True) for score in scores]
+        if pair > 0:
+            before = [run_max[b, g, hl] for hl in heads]
+            tops = [jnp.maximum(old, top) for old, top in zip(before, tops)]
+        expos = [jnp.exp2(score - top) for score, top in zip(scores, tops)]
+        updates = [
+            jnp.dot(
+                expos[hl].astype(jnp.bfloat16),
+                kv[b, g, 1, keys, inner(hl)],
+                preferred_element_type=jnp.float32,
+            )
+            for hl in heads
+        ]
+        totals = [jnp.sum(expo, axis=1, keepdims=True) for expo in expos]
+        if pair > 0:
+            rescales = [jnp.exp2(old - top) for old, top in zip(before, tops)]
+            totals = [run_total[b, g, hl] * rescales[hl] + totals[hl] for hl in heads]
+            updates = [acc[b, g, :, inner(hl)] * rescales[hl] + updates[hl] for hl in heads]
+        if pair < PAIRS - 1:
+            for hl in heads:
+                run_max[b, g, hl] = jnp.broadcast_to(tops[hl], (rows, HEAD_DIM))
+                run_total[b, g, hl] = jnp.broadcast_to(totals[hl], (rows, HEAD_DIM))
+                acc[b, g, :, inner(hl)] = updates[hl]
+        else:
+            energy = squares[pl.ds(b * rows, rows), :]
+            for hl in heads:
+                attended = updates[hl] / totals[hl]
+                acc[b, g, :, inner(hl)] = attended
+                energy = energy + attended * attended
+            squares[pl.ds(b * rows, rows), :] = energy
 
     squares[...] = jnp.zeros_like(squares)
+    work = {2: ((0, 0),), 3: ((0, 1),), 4: ((1, 0), (1, 1))}
     for d in range(1, REACH):
 
         def relay(g, carry):
             arrive(g, d)
             launch(g, d + 1)
+            for pair, b in work.get(d, ()):
+                attend(pair, b, g)
             return carry
 
         lax.fori_loop(0, groups, relay, 0)
-        if d % 2 == 1:
-
-            def work(g, carry):
-                for b in range(2):
-                    attend(d // 2, b, g)
-                return carry
-
-            lax.fori_loop(0, groups, work, 0)
 
     def finish(g, carry):
         arrive(g, REACH)
@@ -387,6 +418,8 @@
     inverse = lax.rsqrt(whole / (width * n_dp) + 1e-06)
     inv_norm[...] = jnp.transpose(jnp.broadcast_to(inverse[0:1], inv_norm.shape))
 
+    load_small[2].wait()
+
     def norm(g, carry):
         for b in range(2):
             factor = inv_norm[pl.ds(b * rows, rows), :]
@@ -411,13 +444,17 @@
         functools.partial(kernel, n_ctx, n_dp),
         out_shape=jax.ShapeDtypeStruct((2, rows, width), jnp.bfloat16),
         in_specs=[
-            pl.BlockSpec(memory_space=pl.ANY),
-            vmem,
-            vmem,
-            pl.BlockSpec(memory_space=pltpu.SMEM),
+            pl.BlockSpec(memory_space=pltpu.HBM),
+            pl.BlockSpec(memory_space=pltpu.HBM),
+            pl.BlockSpec(memory_space=pltpu.HBM),
+            pl.BlockSpec(memory_space=pltpu.HBM),
         ],
         out_specs=vmem,
         scratch_shapes=[
+            pltpu.VMEM(filters.shape, jnp.float32),
+            pltpu.VMEM((1, width), jnp.float32),
+            pltpu.SMEM(doc_lengths.shape, jnp.int32),
+            pltpu.VMEM((9, 8, filters.shape[2]), jnp.float32),
             pltpu.VMEM((2, 3, rows, width), jnp.bfloat16),
             pltpu.VMEM((2, 3, RIM + rows, width), jnp.float32),
             pltpu.VMEM((3, 8, width), jnp.float32),
@@ -432,7 +469,7 @@
             pltpu.VMEM((8, 2 * rows), jnp.float32),
             pltpu.VMEM((n_dp - 1, 8, 2 * rows), jnp.float32),
             pltpu.VMEM((2, rows, HEAD_DIM), jnp.int32),
-            pltpu.SemaphoreType.DMA((4,)),
+            pltpu.SemaphoreType.DMA((7,)),
             pltpu.SemaphoreType.DMA((2,)),
             pltpu.SemaphoreType.DMA((2,)),
             pltpu.SemaphoreType.DMA((2, REACH, groups)),
@@ -441,7 +478,7 @@
             pltpu.SemaphoreType.DMA((n_dp - 1,)),
         ],
         compiler_params=pltpu.CompilerParams(
-            collective_id=0, has_side_effects=True, vmem_limit_bytes=48 * 1024 * 1024
+            collective_id=0, has_side_effects=True, vmem_limit_bytes=67043328
         ),
     )(blocks, filters, gain[None, :], doc_lengths)
     return out[None]

time: 59.8 us -> 43.2 us (0.72)
  Pallas kernels: 55.2 us -> 40.5 us
  local copies, waits for them, and re-layouts: 4.26 us -> 1.88 us
    pallas_call x1, Pallas kernels: 55.2 us -> 40.5 us  [local(): pl.pallas_call(functools.partial(kernel, n_ctx, n_dp), out_shape=jax.Shap...]
    unnamed x9 -> x1, local copies, waits for them, and re-layouts: 4.26 us -> 1.88 us
where the time goes in v2:
time: 43.2 us; the launch traced here: 42.4 us
  Pallas kernels  40.5 us (94%)
  local copies, waits for them, and re-layouts  1.88 us (4%)
    pallas_call x1, Pallas kernels, local(): pl.pallas_call(functools.partial(kernel, n_ctx, n_dp), out_shape=jax.Shap...  40.5 us
    unnamed x1, local copies, waits for them, and re-layouts  1.88 us

profile of v2, /device:TPU:24, one launch (start us, length us, event | category | flops | bytes accessed | tf_op | source)
XLA Modules:
  0.0 42.4 jit_solution(14224971936818366228)
XLA Ops:
  0.0 40.5 %shard_map.46 = bf16[2,64,2048]{2,1,0:T(8,128)(2,1)} custom-call(bf16[2,3,64,2048]{3,2,1,0:T(8,128)(2,1)} %bitcast.6, f32[3,7,128]{2,1,0:T(8,128)} %f_hbm.1, f32[1,2048]{1,0:T(1,128)} %bitcast.7, s32[4]{0:T(128)} %docs_hbm.1), custom_call_target="tpu_custom_call" | custom-call | tf_op jit(solution)/shard_map/pallas_call | solution.py:443
  40.5 1.9 %copy.6 = bf16[1,2,64,2048]{3,2,1,0:T(8,128)(2,1)} copy(bf16[1,2,64,2048]{3,2,1,0:T(8,128)(2,1)} %bitcast.5) | data formatting | bytes 1048576

commit v3 on v2

--- a/solution.py
+++ b/solution.py
@@ -22,11 +22,10 @@
     n_dp,
     x_ref,
     f_hbm,
-    gain_hbm,
     docs_hbm,
     out_ref,
+    inv_norm,
     f_ref,
-    gain_ref,
     docs_ref,
     parts,
     xs,
@@ -39,11 +38,12 @@
     run_total,
     acc,
     squares,
-    inv_norm,
     sq_own,
     sq_peer,
     starts,
     load_sem,
+    out_sem,
+    small_sem,
     halo_send,
     halo_recv,
     kv_send,
@@ -65,20 +65,34 @@
     has_right = place < n_ctx - 1
     is_last = place == n_ctx - 1
 
-    load_kv = [
-        pltpu.make_async_copy(x_ref.at[b, pl.ds(1, 2)], xs.at[b, pl.ds(1, 2)], load_sem.at[b])
-        for b in range(2)
+    def load(g, b, first, count):
+        lanes = pl.ds(g * group_width, group_width)
+        return pltpu.make_async_copy(
+            x_ref.at[b, pl.ds(first, count), :, lanes],
+            xs.at[b, pl.ds(first, count), :, lanes],
+            load_sem.at[b, min(first, 1), g],
+        )
+
+    def load_wait(g, b, first, count):
+        lanes = pl.ds(pl.multiple_of(g * group_width, group_width), group_width)
+        pltpu.make_async_copy(
+            x_ref.at[b, pl.ds(first, count), :, lanes],
+            xs.at[b, pl.ds(first, count), :, lanes],
+            load_sem.at[b, min(first, 1), g],
+        ).wait()
+
+    load_small = [
+        pltpu.make_async_copy(f_hbm, f_ref, small_sem.at[0]),
+        pltpu.make_async_copy(docs_hbm, docs_ref, small_sem.at[1]),
     ]
-    load_q = [
-        pltpu.make_async_copy(x_ref.at[b, 0], xs.at[b, 0], load_sem.at[2 + b]) for b in range(2)
-    ]
-    load_small = [
-        pltpu.make_async_copy(f_hbm, f_ref, load_sem.at[4]),
-        pltpu.make_async_copy(docs_hbm, docs_ref, load_sem.at[5]),
-        pltpu.make_async_copy(gain_hbm, gain_ref, load_sem.at[6]),
-    ]
-    for copy in load_small + load_kv + load_q:
+    for copy in load_small:
         copy.start()
+    for g in range(groups):
+        for b in range(2):
+            load(g, b, 1, 2).start()
+    for g in range(groups):
+        for b in range(2):
+            load(g, b, 0, 1).start()
 
     barrier = pltpu.get_barrier_semaphore()
 
@@ -109,6 +123,9 @@
     rim_fold = pltpu.make_async_copy(
         x_ref.at[0, :, pl.ds(rows - RIM, RIM), :], halo.at[1], halo_recv.at[1]
     )
+    def channel(g, hl):
+        return pl.ds(pl.multiple_of(g * group_width + hl * HEAD_DIM, HEAD_DIM), HEAD_DIM)
+
     spread_shape = (f_ref.shape[2], HEAD_DIM)
     spread_row = lax.broadcasted_iota(jnp.int32, spread_shape, 0)
     spread_col = lax.broadcasted_iota(jnp.int32, spread_shape, 1)
@@ -122,18 +139,20 @@
             parts[3 * part + m, pl.ds(0, taps), :] = piece
             left_over = left_over - piece
     split = parts[...].reshape(72, f_ref.shape[2]).astype(jnp.bfloat16)
-    for h in range(width // HEAD_DIM):
-        first = h * HEAD_DIM
-        hot = (spread_row * group_size <= first + spread_col) & (
-            first + spread_col < (spread_row + 1) * group_size
-        )
-        spread = jnp.dot(
-            split,
-            jnp.where(hot, 1.0, 0.0).astype(jnp.bfloat16),
-            preferred_element_type=jnp.float32,
-        ).reshape(9, 8, HEAD_DIM)
-        for m in range(3):
-            fw[m, :, pl.ds(first, HEAD_DIM)] = (spread[m] + spread[3 + m]) + spread[6 + m]
+
+    def spread_taps(g):
+        for hl in range(group_heads):
+            first = g * group_width + hl * HEAD_DIM
+            hot = (spread_row * group_size <= first + spread_col) & (
+                first + spread_col < (spread_row + 1) * group_size
+            )
+            spread = jnp.dot(
+                split,
+                jnp.where(hot, 1.0, 0.0).astype(jnp.bfloat16),
+                preferred_element_type=jnp.float32,
+            ).reshape(9, 8, HEAD_DIM)
+            for m in range(3):
+                fw[m, :, channel(g, hl)] = (spread[m] + spread[3 + m]) + spread[6 + m]
 
     pl.semaphore_wait(barrier, n_dp - 1 + has_left.astype(jnp.int32) + has_right.astype(jnp.int32))
 
@@ -155,9 +174,6 @@
             term = fw[m, pl.ds(s, 1), lanes] * xf[b, m, pl.ds(first + RIM - taps + 1 + s, count), lanes]
             total = term if total is None else total + term
         return total.astype(jnp.bfloat16)
-
-    def channel(g, hl):
-        return pl.ds(pl.multiple_of(g * group_width + hl * HEAD_DIM, HEAD_DIM), HEAD_DIM)
 
     def inner(hl):
         return pl.ds(hl * HEAD_DIM, HEAD_DIM)
@@ -209,10 +225,10 @@
         def _():
             folded(g, d).wait()
 
-    for copy in load_kv:
-        copy.wait()
-
     def body_rows(g, carry):
+        spread_taps(g)
+        for b in range(2):
+            load_wait(g, b, 1, 2)
         for b in range(2):
             for m in (1, 2):
                 for hl in range(group_heads):
@@ -286,30 +302,29 @@
         )
         starts[b] = begin
 
-    for copy in load_q:
-        copy.wait()
-
-    def query_rows(i, carry):
-        b, g = lax.div(i, groups), lax.rem(i, groups)
-        for hl in range(group_heads):
-            lanes = channel(g, hl)
-            xf[b, 0, pl.ds(0, RIM), lanes] = halo[b, 0, :, lanes].astype(jnp.float32)
-            xf[b, 0, pl.ds(RIM, rows), lanes] = xs[b, 0, :, lanes].astype(jnp.float32)
-        for hl in range(group_heads):
-            qb[b, g, :, inner(hl)] = convolved(b, 0, channel(g, hl), 0, rows)
+    def query_rows(g, carry):
+        for b in range(2):
+            load_wait(g, b, 0, 1)
+            for hl in range(group_heads):
+                lanes = channel(g, hl)
+                xf[b, 0, pl.ds(0, RIM), lanes] = halo[b, 0, :, lanes].astype(jnp.float32)
+                xf[b, 0, pl.ds(RIM, rows), lanes] = xs[b, 0, :, lanes].astype(jnp.float32)
+            for hl in range(group_heads):
+                qb[b, g, :, inner(hl)] = convolved(b, 0, channel(g, hl), 0, rows)
         return carry
 
-    lax.fori_loop(0, 2 * groups, query_rows, 0)
+    lax.fori_loop(0, groups, query_rows, 0)
 
     key_lane = lax.broadcasted_iota(jnp.int32, (rows, HEAD_DIM), 1)
     key_offset = jnp.where(key_lane >= rows, key_lane - 2 * rows, key_lane)
     span = 2 * rows
 
-    def attend(pair, b, g):
-        block = place * rows if b == 0 else (2 * n_ctx - 1 - place) * rows
-        key_pos = key_offset + (block - pair * span)
-        allowed = (key_pos >= starts[b]) & (key_pos <= block + offsets)
-        heads = range(group_heads)
+    def attend(pair, g):
+        allowed = []
+        for b in range(2):
+            key_pos = key_offset + (block_start[b] - pair * span)
+            allowed.append((key_pos >= starts[b]) & (key_pos <= block_start[b] + offsets))
+        units = [(b, hl) for b in range(2) for hl in range(group_heads)]
         keys = pl.ds(pair * span, span)
         scores = [
             lax.dot_general(
@@ -318,57 +333,71 @@
                 (((1,), (1,)), ((), ())),
                 preferred_element_type=jnp.float32,
             )
-            for hl in heads
+            for b, hl in units
         ]
-        scores = [jnp.where(allowed, score * LOG2_SCALE, -1e30) for score in scores]
+        scores = [
+            jnp.where(allowed[b], score * LOG2_SCALE, -1e30)
+            for score, (b, _) in zip(scores, units)
+        ]
         tops = [jnp.max(score, axis=1, keepdims=True) for score in scores]
         if pair > 0:
-            before = [run_max[b, g, hl] for hl in heads]
+            before = [run_max[b, g, hl] for b, hl in units]
             tops = [jnp.maximum(old, top) for old, top in zip(before, tops)]
         expos = [jnp.exp2(score - top) for score, top in zip(scores, tops)]
         updates = [
             jnp.dot(
-                expos[hl].astype(jnp.bfloat16),
+                expo.astype(jnp.bfloat16),
                 kv[b, g, 1, keys, inner(hl)],
                 preferred_element_type=jnp.float32,
             )
-            for hl in heads
+            for expo, (b, hl) in zip(expos, units)
         ]
         totals = [jnp.sum(expo, axis=1, keepdims=True) for expo in expos]
         if pair > 0:
             rescales = [jnp.exp2(old - top) for old, top in zip(before, tops)]
-            totals = [run_total[b, g, hl] * rescales[hl] + totals[hl] for hl in heads]
-            updates = [acc[b, g, :, inner(hl)] * rescales[hl] + updates[hl] for hl in heads]
+            totals = [
+                run_total[b, g, hl] * rescale + total
+                for total, rescale, (b, hl) in zip(totals, rescales, units)
+            ]
+            updates = [
+                acc[b, :, channel(g, hl)] * rescale + update
+                for update, rescale, (b, hl) in zip(updates, rescales, units)
+            ]
         if pair < PAIRS - 1:
-            for hl in heads:
-                run_max[b, g, hl] = jnp.broadcast_to(tops[hl], (rows, HEAD_DIM))
-                run_total[b, g, hl] = jnp.broadcast_to(totals[hl], (rows, HEAD_DIM))
-                acc[b, g, :, inner(hl)] = updates[hl]
+            for top, total, update, (b, hl) in zip(tops, totals, updates, units):
+                run_max[b, g, hl] = jnp.broadcast_to(top, (rows, HEAD_DIM))
+                run_total[b, g, hl] = jnp.broadcast_to(total, (rows, HEAD_DIM))
+                acc[b, :, channel(g, hl)] = update
         else:
-            energy = squares[pl.ds(b * rows, rows), :]
-            for hl in heads:
-                attended = updates[hl] / totals[hl]
-                acc[b, g, :, inner(hl)] = attended
-                energy = energy + attended * attended
-            squares[pl.ds(b * rows, rows), :] = energy
+            for total, update, (b, hl) in zip(totals, updates, units):
+                attended = update / total
+                acc[b, :, channel(g, hl)] = attended
+                squares[pl.ds(b * rows, rows), :] += attended * attended
 
     squares[...] = jnp.zeros_like(squares)
-    work = {2: ((0, 0),), 3: ((0, 1),), 4: ((1, 0), (1, 1))}
+    work = {2: 0, 4: 1}
     for d in range(1, REACH):
 
         def relay(g, carry):
             arrive(g, d)
             launch(g, d + 1)
-            for pair, b in work.get(d, ()):
-                attend(pair, b, g)
+            if d in work:
+                attend(work[d], g)
             return carry
 
         lax.fori_loop(0, groups, relay, 0)
+
+    def given(g, b):
+        lanes = pl.ds(pl.multiple_of(g * group_width, group_width), group_width)
+        return pltpu.make_async_copy(
+            acc.at[b, :, lanes], out_ref.at[b, :, lanes], out_sem.at[b, g]
+        )
 
     def finish(g, carry):
         arrive(g, REACH)
-        for b in range(2):
-            attend(PAIRS - 1, b, g)
+        attend(PAIRS - 1, g)
+        for b in range(2):
+            given(g, b).start()
         return carry
 
     lax.fori_loop(0, groups, finish, 0)
@@ -418,41 +447,35 @@
     inverse = lax.rsqrt(whole / (width * n_dp) + 1e-06)
     inv_norm[...] = jnp.transpose(jnp.broadcast_to(inverse[0:1], inv_norm.shape))
 
-    load_small[2].wait()
-
-    def norm(g, carry):
-        for b in range(2):
-            factor = inv_norm[pl.ds(b * rows, rows), :]
-            for hl in range(group_heads):
-                lanes = channel(g, hl)
-                out_ref[b, :, lanes] = (
-                    acc[b, g, :, inner(hl)] * factor * gain_ref[:, lanes]
-                ).astype(jnp.bfloat16)
+    def settle(g, carry):
+        for b in range(2):
+            given(g, b).wait()
         return carry
 
-    lax.fori_loop(0, groups, norm, 0)
+    lax.fori_loop(0, groups, settle, 0)
 
 
 def local(n_ctx, n_dp, projected, filters, gain, doc_lengths):
     blocks = jnp.transpose(projected[0], (0, 2, 1, 3))
     rows, width = blocks.shape[2], blocks.shape[3]
-    group_width = min(width, 4 * HEAD_DIM)
+    group_width = min(width, 2 * HEAD_DIM)
     groups = width // group_width
     group_heads = group_width // HEAD_DIM
     vmem = pl.BlockSpec(memory_space=pltpu.VMEM)
-    out = pl.pallas_call(
+    attended, inverse = pl.pallas_call(
         functools.partial(kernel, n_ctx, n_dp),
-        out_shape=jax.ShapeDtypeStruct((2, rows, width), jnp.bfloat16),
+        out_shape=(
+            jax.ShapeDtypeStruct((2, rows, width), jnp.float32),
+            jax.ShapeDtypeStruct((2 * rows, HEAD_DIM), jnp.float32),
+        ),
         in_specs=[
             pl.BlockSpec(memory_space=pltpu.HBM),
             pl.BlockSpec(memory_space=pltpu.HBM),
             pl.BlockSpec(memory_space=pltpu.HBM),
-            pl.BlockSpec(memory_space=pltpu.HBM),
         ],
-        out_specs=vmem,
+        out_specs=(pl.BlockSpec(memory_space=pltpu.HBM), vmem),
         scratch_shapes=[
             pltpu.VMEM(filters.shape, jnp.float32),
-            pltpu.VMEM((1, width), jnp.float32),
             pltpu.SMEM(doc_lengths.shape, jnp.int32),
             pltpu.VMEM((9, 8, filters.shape[2]), jnp.float32),
             pltpu.VMEM((2, 3, rows, width), jnp.bfloat16),
@@ -463,13 +486,14 @@
             pltpu.VMEM((2, groups, 2, (REACH + 1) * rows, group_width), jnp.bfloat16),
             pltpu.VMEM((2, groups, group_heads, rows, HEAD_DIM), jnp.float32),
             pltpu.VMEM((2, groups, group_heads, rows, HEAD_DIM), jnp.float32),
-            pltpu.VMEM((2, groups, rows, group_width), jnp.float32),
-            pltpu.VMEM((2 * rows, HEAD_DIM), jnp.float32),
+            pltpu.VMEM((2, rows, width), jnp.float32),
             pltpu.VMEM((2 * rows, HEAD_DIM), jnp.float32),
             pltpu.VMEM((8, 2 * rows), jnp.float32),
             pltpu.VMEM((n_dp - 1, 8, 2 * rows), jnp.float32),
             pltpu.VMEM((2, rows, HEAD_DIM), jnp.int32),
-            pltpu.SemaphoreType.DMA((7,)),
+            pltpu.SemaphoreType.DMA((2, 2, groups)),
+            pltpu.SemaphoreType.DMA((2, groups)),
+            pltpu.SemaphoreType.DMA((2,)),
             pltpu.SemaphoreType.DMA((2,)),
             pltpu.SemaphoreType.DMA((2,)),
             pltpu.SemaphoreType.DMA((2, REACH, groups)),
@@ -480,8 +504,9 @@
         compiler_params=pltpu.CompilerParams(
             collective_id=0, has_side_effects=True, vmem_limit_bytes=67043328
         ),
-    )(blocks, filters, gain[None, :], doc_lengths)
-    return out[None]
+    )(blocks, filters, doc_lengths)
+    inverse = inverse.reshape(2, rows, HEAD_DIM)[:, :, :1]
+    return (attended * inverse * gain).astype(jnp.bfloat16)[None]
 
 
 def solution(mesh):

time: 43.2 us -> 44.9 us (1.039)
  other arithmetic: 0 us -> 2.18 us
  local copies, waits for them, and re-layouts: 1.88 us -> 0.92 us
  Pallas kernels: 40.5 us -> 41.1 us
    broadcast_in_dim x0 -> x1, other arithmetic: none -> 2.18 us  [local(): return (attended * inverse * gain).astype(jnp.bfloat16)[None]]
    unnamed x1, local copies, waits for them, and re-layouts: 1.88 us -> 0.92 us
    pallas_call x1, Pallas kernels: 40.5 us -> 41.1 us  [local(): pl.pallas_call(functools.partial(kernel, n_ctx, n_dp), out_shape=(jax.Sha...]
where the time goes in v3:
time: 44.9 us; the launch traced here: 44.2 us
  Pallas kernels  41.1 us (92%)
  other arithmetic  2.18 us (5%)
  local copies, waits for them, and re-layouts  0.92 us (2%)
    pallas_call x1, Pallas kernels, local(): pl.pallas_call(functools.partial(kernel, n_ctx, n_dp), out_shape=(jax.Sha...  41.1 us
    broadcast_in_dim x1, other arithmetic, local(): return (attended * inverse * gain).astype(jnp.bfloat16)[None]  2.18 us
    unnamed x1, local copies, waits for them, and re-layouts  0.92 us

profile of v3, /device:TPU:24, one launch (start us, length us, event | category | flops | bytes accessed | tf_op | source)
XLA Modules:
  0.0 44.2 jit_solution(4702985451250439233)
XLA Ops:
  0.0 41.1 %shard_map.46 = (f32[2,64,2048]{2,1,0:T(8,128)}, f32[128,128]{1,0:T(8,128)}) custom-call(bf16[2,3,64,2048]{3,2,1,0:T(8,128)(2,1)} %bitcast.8, f32[3,7,128]{2,1,0:T(8,128)} %f_hbm.1, s32[4]{0:T(128)} %docs_hbm.1), custom_call_target="tpu_custom_call" | custom-call | tf_op jit(solution)/shard_map/pallas_call | solution.py:465
  41.1 0.9 %copy.6 = f32[2,64,1]{1,0,2:T(2,128)S(1)} copy(f32[2,64,1]{2,1,0:T(8,128)} %bitcast.9) | data formatting | bytes 1024
  42.0 2.2 %fusion = bf16[1,2,64,2048]{3,2,1,0:T(8,128)(2,1)} fusion(f32[2,64,2048]{2,1,0:T(8,128)} %get-tuple-element.7, f32[2048]{0:T(1024)} %param.6, f32[2,64]{1,0:T(2,128)S(1)} %bitcast.10), kind=kLoop, calls=%fused_computation.1 | loop fusion | flops 786432 | bytes 1581568 | tf_op jit(solution)/shard_map/broadcast_in_dim | solution.py:509
